TPU v7x, 32 devices: a whole 2x2x4 slice. The times are simulated.
32 devices in a mesh: row: 4 (over y, core), col: 8 (over z, x).
Axes of the slice: x: 2, y: 2, z: 4, core: 2. Of those that a mesh axis runs over, the one named last changes fastest.
Arguments:
- probes: float32 [32768, 256], P(('row', 'col')), may hold values from -6 to 6
- near_blocks: bfloat16 [32, 8, 1024, 1024], P(('row', 'col')), may hold values from -0.09375 to 0.09375
- near_leaves: int32 [32, 8], P(('row', 'col')), may hold values from 0 to 7, as said below
- near_count: int32 [32], P(('row', 'col')), may hold values from 1 to 8, as said below
- leaf_rank: int32 [32], P(('row', 'col')), may hold values from 128 to 256
- leaf_basis: float32 [32768, 256], P(('row', 'col')), may hold values from -0.1875 to 0.1875
- leaf_transfer: float32 [32, 256, 512], P(('row', 'col')), may hold values from -0.125 to 0.125
- leaf_links: int32 [32, 4], P(('row', 'col')), may hold values from 0 to 7, as said below
- leaf_link_blocks: float32 [32, 4, 256, 256], P(('row', 'col')), may hold values from -0.1875 to 0.1875
- parent_links: int32 [4, 2], P('row'), may hold values from 0 to 3, as said below
- parent_link_blocks: float32 [4, 2, 512, 512], P('row'), may hold values from -0.1875 to 0.1875
Outputs:
- term_one: float32 [32768, 256], P(('row', 'col'))
- term_two: float32 [32768, 256], P(('row', 'col'))
Inputs may be any that keep to these rules, and one draw needn't show every extreme that they name: `near_leaves`: slot 0 of every leaf is the leaf's own position; slots 1 to near_count - 1 are distinct other positions of the same group; later slots repeat the leaf's own position. `near_count`: some leaf has 8 live slots in every draw. `leaf_links`: each leaf's 4 coupled positions are distinct and differ from its own. `parent_links`: each parent's 2 coupled parents are distinct and differ from itself.
All inputs are finite; a program needn't handle non-finite values.
Results may differ from a plain program's by a relative error of at most 0.0034.
Values may be sent and summed in bfloat16 or wider, within the bound.
No kernel may reach another device: no remote copies, remote signals or barrier semaphores. Data moves between devices by JAX's collectives and lax.ppermute only.
A program may use at most 128 MiB of HBM per device.

v0:
```python
import jax
import jax.numpy as jnp
from jax import lax
from jax.sharding import PartitionSpec as P


def local(
    probes,
    near_blocks,
    near_leaves,
    near_count,
    leaf_rank,
    leaf_basis,
    leaf_transfer,
    leaf_links,
    leaf_link_blocks,
    parent_links,
    parent_link_blocks,
):
    highest = lax.Precision.HIGHEST
    span_col = lax.axis_size("col")
    span_row = lax.axis_size("row")
    leaf_rows = probes.shape[0]
    probe_cols = probes.shape[1]
    rank_cols = leaf_basis.shape[1]
    parent_cols = leaf_transfer.shape[2]
    rank_mask = (jnp.arange(rank_cols, dtype=jnp.int32) < leaf_rank[0]).astype(jnp.float32)[:, None]
    transfer = leaf_transfer[0]
    own_blocks = near_blocks[0]
    own_near = near_leaves[0]

    def multiply(vector):
        packed = vector.astype(jnp.bfloat16)
        empty = jnp.zeros((leaf_rows, probe_cols), jnp.float32)
        stacked = lax.all_gather(packed, "col", axis=0, tiled=True).reshape(
            span_col, leaf_rows, probe_cols
        )

        def add_slot(slot, total):
            near_block = lax.dynamic_index_in_dim(own_blocks, slot, 0, False)
            source = lax.dynamic_index_in_dim(stacked, own_near[slot], 0, False)
            return total + jnp.dot(near_block, source, preferred_element_type=jnp.float32)

        near_sum = lax.fori_loop(0, near_count[0], add_slot, empty)
        skeleton = jnp.dot(leaf_basis.T, vector, precision=highest) * rank_mask
        gathered = lax.all_gather(skeleton, "col", axis=0, tiled=True).reshape(
            span_col, rank_cols, probe_cols
        )
        linked = gathered[leaf_links[0]]
        coupled = jnp.einsum("kab,kbp->ap", leaf_link_blocks[0], linked, precision=highest)
        upward = jnp.dot(transfer.T, skeleton, precision=highest)
        portion = lax.psum_scatter(upward, "col", scatter_dimension=1, tiled=True)
        every_parent = lax.all_gather(portion, "row", axis=0, tiled=True).reshape(
            span_row, parent_cols, -1
        )
        far_portion = jnp.einsum(
            "kab,kbp->ap", parent_link_blocks[0], every_parent[parent_links[0]], precision=highest
        )
        far_parent = lax.all_gather(far_portion, "col", axis=1, tiled=True)
        combined = (coupled + jnp.dot(transfer, far_parent, precision=highest)) * rank_mask
        return jnp.dot(leaf_basis, combined, precision=highest) + near_sum

    term_one = multiply(probes)
    term_two = 2.0 * multiply(term_one) - probes
    return (term_one, term_two)


def solution(mesh):
    in_specs = (
        P(("row", "col"), None),
        P(("row", "col"), None, None, None),
        P(("row", "col"), None),
        P(("row", "col")),
        P(("row", "col")),
        P(("row", "col"), None),
        P(("row", "col"), None, None),
        P(("row", "col"), None),
        P(("row", "col"), None, None, None),
        P("row", None),
        P("row", None, None, None),
    )
    out_specs = (P(("row", "col"), None), P(("row", "col"), None))
    return jax.shard_map(local, mesh=mesh, in_specs=in_specs, out_specs=out_specs, check_vma=False)
```

profile of v0, /device:TPU:4, one launch (start us, length us, event | category | flops | bytes accessed | tf_op | source)
XLA Modules:
  0.0 513.7 jit_solution(4543359432863506335)
XLA Ops:
  8.0 3.5 convolution_multiply_fusion.1
  11.5 2.6 convolution_bitcast_fusion.3
  14.2 0.7 all-gather.5.cloned.1.call-update
  14.9 0.8 convert_element_type.14
  15.9 62.3 %reduce-scatter.3.cloned.1.call-done = f32[512,32]{0,1:T(8,128)} async-done(((f32[512,256]{0,1:T(8,128)}), f32[512,32]{0,1:T(8,128)}) %reduce-scatter.3.cloned.1.call-update) | async-done | bytes 65552 | tf_op jit(solution)/shard_map/reduce_scatter | solution.py:52
  78.2 6.0 %all_gather.25 = f32[2048,32]{0,1:T(8,128)S(1)} all-gather(f32[512,32]{0,1:T(8,128)} %reduce-scatter.3.cloned.1.call-done), channel_id=1, replica_groups=mesh['row'=4,'col'=8] {'row'}, dimensions={0}, use_global_device_ids=true | all-gather | bytes 327680 | tf_op jit(solution)/shard_map/all_gather | solution.py:53
  84.8 2.0 fusion.28
  86.8 32.8 %all_gather.26 = f32[512,256]{0,1:T(8,128)S(1)} all-gather(f32[512,32]{0,1:T(8,128)S(1)} %fusion.28), channel_id=1, replica_groups=mesh['row'=4,'col'=8] {'col'}, dimensions={1}, use_global_device_ids=true | all-gather | bytes 589824 | tf_op jit(solution)/shard_map/all_gather | solution.py:59
  119.6 11.7 %all-gather.5.cloned.1.call-done = f32[2048,256]{1,0:T(8,128)} async-done(((f32[256,256]{1,0:T(8,128)}), f32[2048,256]{1,0:T(8,128)}) %all-gather.5.cloned.1.call-update) | async-done | bytes 2097168 | tf_op jit(solution)/shard_map/all_gather | solution.py:46
  131.3 3.2 gather_fusion
  134.5 3.4 convolution_bitcast_fusion.5
  137.9 0.6 fusion.26
  138.5 68.2 %all-gather.7.cloned.1.call-done = bf16[8192,256]{1,0:T(8,128)(2,1)} async-done(((bf16[1024,256]{1,0:T(8,128)(2,1)}), bf16[8192,256]{1,0:T(8,128)(2,1)}) %all-gather.7.cloned.1.call-update) | async-done | bytes 4194320 | tf_op jit(solution)/shard_map/all_gather | solution.py:35
  206.8 45.6 %while.20 = (s32[]{:T(128)}, f32[1024,256]{1,0:T(8,128)S(1)}, s32[]{:T(128)}, bf16[8,1024,1024]{2,1,0:T(8,128)(2,1)}, s32[8]{0:T(128)S(1)}, /*index=5*/bf16[8,10...) while((s32[]{:T(128)}, f32[1024,256]{1,0:T(8,128)S(1)}, s32[]{:T(128)}, ...), condition=%wide.region_2.3_spmd, body=%wide.region_1.2_spmd.sunk | while | flops 537133056 | bytes 4718773 | solution.py:44
  207.4 0.6 dynamic_slice.48
  210.0 2.4 fusion.67
  213.0 0.6 dynamic_slice.48
  215.6 2.4 fusion.67
  218.7 0.6 dynamic_slice.48
  221.2 2.4 fusion.67
  224.3 0.6 dynamic_slice.48
  226.8 2.4 fusion.67
  229.9 0.6 dynamic_slice.48
  232.4 2.4 fusion.67
  235.5 0.6 dynamic_slice.48
  238.1 2.4 fusion.67
  241.1 0.6 dynamic_slice.48
  243.7 2.4 fusion.67
  246.8 0.6 dynamic_slice.48
  249.3 2.4 fusion.67
  252.4 1.3 copy.20
  253.7 3.5 fusion.42
  257.2 1.0 convolution_multiply_fusion
  258.6 1.4 convolution_bitcast_fusion.2
  261.2 1.4 copy.25
  262.6 2.5 copy.26
  265.1 55.6 %reduce-scatter.5.cloned.1.call-done = f32[512,32]{0,1:T(8,128)} async-done(((f32[512,256]{0,1:T(8,128)}), f32[512,32]{0,1:T(8,128)}) %reduce-scatter.5.cloned.1.call-update) | async-done | bytes 65552 | tf_op jit(solution)/shard_map/reduce_scatter | solution.py:52
  320.7 6.0 %all_gather.29 = f32[2048,32]{0,1:T(8,128)S(1)} all-gather(f32[512,32]{0,1:T(8,128)} %reduce-scatter.5.cloned.1.call-done), channel_id=1, replica_groups=mesh['row'=4,'col'=8] {'row'}, dimensions={0}, use_global_device_ids=true | all-gather | bytes 327680 | tf_op jit(solution)/shard_map/all_gather | solution.py:53
  327.3 2.0 fusion.31
  329.3 32.8 %all_gather.30 = f32[512,256]{0,1:T(8,128)S(1)} all-gather(f32[512,32]{0,1:T(8,128)S(1)} %fusion.31), channel_id=1, replica_groups=mesh['row'=4,'col'=8] {'col'}, dimensions={1}, use_global_device_ids=true | all-gather | bytes 589824 | tf_op jit(solution)/shard_map/all_gather | solution.py:59
  362.1 13.3 %all-gather.9.cloned.1.call-done = f32[2048,256]{0,1:T(8,128)} async-done(((f32[256,256]{0,1:T(8,128)}), f32[2048,256]{0,1:T(8,128)}) %all-gather.9.cloned.1.call-update) | async-done | bytes 2097168 | tf_op jit(solution)/shard_map/all_gather | solution.py:46
  375.4 3.0 copy.28
  378.4 3.2 gather_fusion.2
  381.7 3.4 convolution_bitcast_fusion.4
  385.0 0.6 fusion.27
  385.7 63.5 %all-gather.11.cloned.1.call-done = bf16[8192,256]{0,1:T(8,128)(2,1)} async-done(((bf16[1024,256]{0,1:T(8,128)(2,1)}), bf16[8192,256]{0,1:T(8,128)(2,1)}) %all-gather.11.cloned.1.call-update) | async-done | bytes 4194320 | tf_op jit(solution)/shard_map/all_gather | solution.py:35
  449.2 6.5 %copy.29 = bf16[8192,256]{1,0:T(8,128)(2,1)} copy(bf16[8192,256]{0,1:T(8,128)(2,1)} %all-gather.11.cloned.1.call-done) | data formatting | bytes 8388608 | tf_op jit(solution)/shard_map/while | solution.py:44
  455.7 45.6 %while.21 = (s32[]{:T(128)}, f32[1024,256]{1,0:T(8,128)S(1)}, s32[]{:T(128)}, bf16[8,1024,1024]{2,1,0:T(8,128)(2,1)}, s32[8]{0:T(128)S(1)}, /*index=5*/bf16[8,10...) while((s32[]{:T(128)}, f32[1024,256]{1,0:T(8,128)S(1)}, s32[]{:T(128)}, ...), condition=%wide.region_5.6_spmd, body=%wide.region_4.5_spmd.sunk | while | flops 537133056 | bytes 4718773 | solution.py:44
  458.9 2.4 fusion.70
  462.0 0.6 dynamic_slice.51
  464.5 2.4 fusion.70
  467.6 0.6 dynamic_slice.51
  470.2 2.4 fusion.70
  473.3 0.6 dynamic_slice.51
  475.8 2.4 fusion.70
  481.4 2.4 fusion.70
  484.5 0.6 dynamic_slice.51
  487.0 2.4 fusion.70
  490.1 0.6 dynamic_slice.51
  492.6 2.4 fusion.70
  498.3 2.4 fusion.70
  501.3 1.3 copy.24
  502.6 2.9 fusion.25
  505.6 1.3 copy.27
  (51 shorter events, 4.8 us)
Async XLA Ops:
  7.2 77.6 %copy-start = (f32[1,2,512,512]{3,2,1,0:T(8,128)S(1)}, f32[1,2,512,512]{3,2,1,0:T(8,128)}, u32[]{:S(2)}) copy-start(f32[1,2,512,512]{3,2,1,0:T(8,128)} %param.25) | copy-start | bytes 6291460
  7.2 71.1 %reduce-scatter.3.cloned.1.call-start = ((), (), s32[]{:S(2)}) async-start(), calls=%async_computation.3 | async-start | bytes 589824 | tf_op jit(solution)/shard_map/reduce_scatter | solution.py:52
  8.0 6.9 %copy-start.2 = (f32[1024,256]{1,0:T(8,128)S(1)}, f32[1024,256]{1,0:T(8,128)}, u32[]{:S(2)}) copy-start(f32[1024,256]{1,0:T(8,128)} %param.15) | copy-start | bytes 3145732
  11.5 2.7 copy-start.8
  11.5 4.3 copy-start.10
  11.5 4.4 copy-start.11
  14.1 117.2 %all-gather.5.cloned.1.call-start = ((), (), s32[]{:S(2)}) async-start(), calls=%async_computation.2 | async-start | bytes 2359296 | tf_op jit(solution)/shard_map/all_gather | solution.py:46
  14.9 191.8 %all-gather.7.cloned.1.call-start = ((), (), s32[]{:S(2)}) async-start(), calls=%async_computation.4 | async-start | bytes 4718592 | tf_op jit(solution)/shard_map/all_gather | solution.py:35
  15.8 304.9 %reduce-scatter.5.cloned.1.call-start = ((), (), s32[]{:S(2)}) async-start(), calls=%async_computation.6 | async-start | bytes 589824 | tf_op jit(solution)/shard_map/reduce_scatter | solution.py:52
  131.3 6.6 %copy-start.5 = (f32[1,256,512]{2,1,0:T(8,128)S(1)}, f32[1,256,512]{2,1,0:T(8,128)}, u32[]{:S(2)}) copy-start(f32[1,256,512]{2,1,0:T(8,128)} %param.21) | copy-start | bytes 1572868
  134.5 72.2 %copy-start.12 = (s32[1,8]{1,0:T(1,128)S(1)}, s32[1,8]{1,0:T(1,128)}, u32[]{:S(2)}) copy-start(s32[1,8]{1,0:T(1,128)} %param.17) | copy-start | bytes 100
  253.7 3.5 copy-start.1
  257.2 1.0 copy-start.4
  257.2 1.4 copy-start.6
  257.2 4.0 copy-start.3
  258.6 1.5 copy-start.9
  260.0 115.4 %all-gather.9.cloned.1.call-start = ((), (), s32[]{:S(2)}) async-start(), calls=%async_computation.5 | async-start | bytes 2359296 | tf_op jit(solution)/shard_map/all_gather | solution.py:46
  260.6 188.6 %all-gather.11.cloned.1.call-start = ((), (), s32[]{:S(2)}) async-start(), calls=%async_computation.7 | async-start | bytes 4718592 | tf_op jit(solution)/shard_map/all_gather | solution.py:35
  378.4 6.6 %copy-start.7 = (f32[1,256,512]{2,1,0:T(8,128)S(1)}, f32[1,256,512]{2,1,0:T(8,128)}, u32[]{:S(2)}) copy-start(f32[1,256,512]{2,1,0:T(8,128)} %param.21) | copy-start | bytes 1572868
Sparse Core Ops, SparseCore 0:
  14.2 63.9 reduce-scatter.2
  80.4 50.8 all-gather.4
  134.0 72.6 all-gather.6
  260.1 60.5 reduce-scatter.4
  322.6 52.8 all-gather.8
  377.5 71.6 all-gather.10
where the time goes:
time: 515 us; the launch traced here: 514 us
  waiting for transfers between devices  276 us (54%)
  blocking collectives  77.6 us (15%)
  matrix products  65.5 us (13%)
  loops' own time  43.2 us (8%)
  local copies, waits for them, and re-layouts  34.8 us (7%)
  between operations  15.2 us (3%)
    all_gather x2, waiting for transfers between devices, multiply(): lax.all_gather(packed, 'col', axis=0, tiled=True)  132 us
    reduce_scatter x2, waiting for transfers between devices, multiply(): portion = lax.psum_scatter(upward, 'col', scatter_dimension=1, tiled=True)  118 us
    all_gather x2, blocking collectives, multiply(): far_parent = lax.all_gather(far_portion, 'col', axis=1, tiled=True)  65.6 us
    another operation x2, loops' own time, multiply(): near_sum = lax.fori_loop(0, near_count[0], add_slot, empty)  43.2 us
    dot_general x16, matrix products, add_slot(): jnp.dot(near_block, source, preferred_element_type=jnp.float32)  38.6 us
    all_gather x2, waiting for transfers between devices, multiply(): lax.all_gather(skeleton, 'col', axis=0, tiled=True)  25 us
    all_gather x2, blocking collectives, multiply(): lax.all_gather(portion, 'row', axis=0, tiled=True)  11.9 us
  transfers between devices with their start and end apart: 6, of which 6 were waited for; matrix products, arithmetic and copies ran while one was open for 5% of the time, Pallas kernels for 0%

commit v1 on v0

--- a/solution.py
+++ b/solution.py
@@ -1,7 +1,25 @@
+import functools
 import jax
 import jax.numpy as jnp
 from jax import lax
 from jax.sharding import PartitionSpec as P
+
+
+def convert_racks(obj, pos_dim):
+    n_dev_all = jax.lax.axis_size("col")
+    vec_out = obj
+    row_list = [vec_out]
+    high = sorted(((ii, (ii + 1) % n_dev_all) for ii in range(n_dev_all)))
+    for idx in range(1, n_dev_all):
+        vec_out = jax.lax.ppermute(vec_out, "col", perm=high)
+        row_list.insert(0, vec_out)
+    clean = jnp.concatenate(row_list, pos_dim)
+    frame_out = jax.lax.axis_index("col")
+    row_out = frame_out + 1
+    return jnp.roll(clean, row_out * obj.shape[pos_dim], pos_dim)
+
+
+_read_loops = functools.partial(convert_racks, pos_dim=1)
 
 
 def local(
@@ -56,7 +74,7 @@
         far_portion = jnp.einsum(
             "kab,kbp->ap", parent_link_blocks[0], every_parent[parent_links[0]], precision=highest
         )
-        far_parent = lax.all_gather(far_portion, "col", axis=1, tiled=True)
+        far_parent = _read_loops(far_portion)
         combined = (coupled + jnp.dot(transfer, far_parent, precision=highest)) * rank_mask
         return jnp.dot(leaf_basis, combined, precision=highest) + near_sum
 

time: 515 us -> 520 us (level)
  blocking collectives: 77.6 us -> 11.9 us
  waiting for transfers between devices: 276 us -> 336 us
  local copies, waits for them, and re-layouts: 34.8 us -> 41.7 us
    ppermute x0 -> x14, waiting for transfers between devices: none -> 105 us  [convert_racks(): vec_out = jax.lax.ppermute(vec_out, 'col', perm=high)]
    all_gather x2 -> x0, blocking collectives: 65.6 us -> none  [multiply(): far_parent = lax.all_gather(far_portion, 'col', axis=1, tiled=True)]
    all_gather x2, waiting for transfers between devices: 25 us -> 0.02 us  [multiply(): lax.all_gather(skeleton, 'col', axis=0, tiled=True)]
    all_gather x2, waiting for transfers between devices: 132 us -> 107 us  [multiply(): lax.all_gather(packed, 'col', axis=0, tiled=True)]
    unnamed x29 -> x43, local copies, waits for them, and re-layouts: 5.65 us -> 11.7 us
  transfers between devices with their start and end apart: 6 -> 20, of which waited for: 6 -> 18; matrix products, arithmetic and copies ran while one was open for 5% -> 7% of each run, Pallas kernels for 0% -> 0%
where the time goes in v1:
time: 520 us; the launch traced here: 519 us
  waiting for transfers between devices  336 us (65%)
  matrix products  66.6 us (13%)
  loops' own time  43.4 us (8%)
  local copies, waits for them, and re-layouts  41.7 us (8%)
  between operations  15.3 us (3%)
  blocking collectives  11.9 us (2%)
    reduce_scatter x2, waiting for transfers between devices, multiply(): portion = lax.psum_scatter(upward, 'col', scatter_dimension=1, tiled=True)  122 us
    all_gather x2, waiting for transfers between devices, multiply(): lax.all_gather(packed, 'col', axis=0, tiled=True)  107 us
    ppermute x14, waiting for transfers between devices, convert_racks(): vec_out = jax.lax.ppermute(vec_out, 'col', perm=high)  105 us
    another operation x2, loops' own time, multiply(): near_sum = lax.fori_loop(0, near_count[0], add_slot, empty)  43.4 us
    dot_general x16, matrix products, add_slot(): jnp.dot(near_block, source, preferred_element_type=jnp.float32)  38.6 us
    all_gather x2, blocking collectives, multiply(): lax.all_gather(portion, 'row', axis=0, tiled=True)  11.9 us
    unnamed x43, local copies, waits for them, and re-layouts  11.7 us
  transfers between devices with their start and end apart: 20, of which 18 were waited for; matrix products, arithmetic and copies ran while one was open for 7% of the time, Pallas kernels for 0%

profile of v1, /device:TPU:4, one launch (start us, length us, event | category | flops | bytes accessed | tf_op | source)
XLA Modules:
  0.0 518.6 jit_solution(10481920622310867863)
XLA Ops:
  8.0 3.5 convolution_multiply_fusion.1
  11.5 2.6 convolution_bitcast_fusion.3
  14.2 0.7 all-gather.5.cloned.1.call-update
  14.9 0.8 convert_element_type.14
  15.9 62.3 %reduce-scatter.3.cloned.1.call-done = f32[512,32]{0,1:T(8,128)} async-done(((f32[512,256]{0,1:T(8,128)}), f32[512,32]{0,1:T(8,128)}) %reduce-scatter.3.cloned.1.call-update) | async-done | bytes 65552 | tf_op jit(solution)/shard_map/reduce_scatter | solution.py:70
  78.2 6.0 %all_gather.19 = f32[2048,32]{0,1:T(8,128)S(1)} all-gather(f32[512,32]{0,1:T(8,128)} %reduce-scatter.3.cloned.1.call-done), channel_id=1, replica_groups=mesh['row'=4,'col'=8] {'row'}, dimensions={0}, use_global_device_ids=true | all-gather | bytes 327680 | tf_op jit(solution)/shard_map/all_gather | solution.py:71
  84.8 2.0 fusion.28
  86.8 1.4 collective-permute-start
  88.2 7.1 %collective-permute-done = f32[512,32]{0,1:T(8,128)S(1)} collective-permute-done((f32[512,32]{0,1:T(8,128)S(1)}, f32[512,32]{0,1:T(8,128)S(1)}, u32[]{:S(2)}, u32[]{:S(2)}) %collective-permute-start) | collective-permute-done | bytes 65568 | tf_op jit(solution)/shard_map/ppermute | solution.py:14
  95.3 8.1 %collective-permute-done.1 = f32[512,32]{0,1:T(8,128)S(1)} collective-permute-done((f32[512,32]{0,1:T(8,128)S(1)}, f32[512,32]{0,1:T(8,128)S(1)}, u32[]{:S(2)}, u32[]{:S(2)}) %collective-permute-start.1) | collective-permute-done | bytes 65568 | tf_op jit(solution)/shard_map/ppermute | solution.py:14
  103.4 7.0 %collective-permute-done.2 = f32[512,32]{0,1:T(8,128)S(1)} collective-permute-done((f32[512,32]{0,1:T(8,128)S(1)}, f32[512,32]{0,1:T(8,128)S(1)}, u32[]{:S(2)}, u32[]{:S(2)}) %collective-permute-start.2) | collective-permute-done | bytes 65568 | tf_op jit(solution)/shard_map/ppermute | solution.py:14
  110.3 8.7 %collective-permute-done.3 = f32[512,32]{0,1:T(8,128)S(1)} collective-permute-done((f32[512,32]{0,1:T(8,128)S(1)}, f32[512,32]{0,1:T(8,128)S(1)}, u32[]{:S(2)}, u32[]{:S(2)}) %collective-permute-start.3) | collective-permute-done | bytes 65568 | tf_op jit(solution)/shard_map/ppermute | solution.py:14
  119.0 8.0 %collective-permute-done.4 = f32[512,32]{0,1:T(8,128)S(1)} collective-permute-done((f32[512,32]{0,1:T(8,128)S(1)}, f32[512,32]{0,1:T(8,128)S(1)}, u32[]{:S(2)}, u32[]{:S(2)}) %collective-permute-start.4) | collective-permute-done | bytes 65568 | tf_op jit(solution)/shard_map/ppermute | solution.py:14
  127.1 8.2 %collective-permute-done.5 = f32[512,32]{0,1:T(8,128)S(1)} collective-permute-done((f32[512,32]{0,1:T(8,128)S(1)}, f32[512,32]{0,1:T(8,128)S(1)}, u32[]{:S(2)}, u32[]{:S(2)}) %collective-permute-start.5) | collective-permute-done | bytes 65568 | tf_op jit(solution)/shard_map/ppermute | solution.py:14
  135.3 7.0 %collective-permute-done.6 = f32[512,32]{0,1:T(8,128)S(1)} collective-permute-done((f32[512,32]{0,1:T(8,128)S(1)}, f32[512,32]{0,1:T(8,128)S(1)}, u32[]{:S(2)}, u32[]{:S(2)}) %collective-permute-start.6) | collective-permute-done | bytes 65568 | tf_op jit(solution)/shard_map/ppermute | solution.py:14
  142.4 3.4 gather_fusion
  145.8 3.4 convolution_bitcast_fusion.5
  149.8 59.0 %all-gather.7.cloned.1.call-done = bf16[8192,256]{1,0:T(8,128)(2,1)} async-done(((bf16[1024,256]{1,0:T(8,128)(2,1)}), bf16[8192,256]{1,0:T(8,128)(2,1)}) %all-gather.7.cloned.1.call-update) | async-done | bytes 4194320 | tf_op jit(solution)/shard_map/all_gather | solution.py:53
  208.9 45.8 %while.20 = (s32[]{:T(128)}, f32[1024,256]{1,0:T(8,128)S(1)}, s32[]{:T(128)}, bf16[8,1024,1024]{2,1,0:T(8,128)(2,1)}, s32[8]{0:T(128)S(1)}, /*index=5*/bf16[8,10...) while((s32[]{:T(128)}, f32[1024,256]{1,0:T(8,128)S(1)}, s32[]{:T(128)}, ...), condition=%wide.region_2.4_spmd, body=%wide.region_1.3_spmd.sunk | while | flops 537133056 | bytes 4718773 | solution.py:62
  212.1 2.4 fusion.73
  217.7 2.4 fusion.73
  223.3 2.4 fusion.73
  229.0 2.4 fusion.73
  234.6 2.4 fusion.73
  240.2 2.4 fusion.73
  245.8 2.4 fusion.73
  251.4 2.4 fusion.73
  254.7 1.3 copy.20
  256.0 3.5 fusion.50
  259.5 1.0 convolution_multiply_fusion
  260.9 1.4 convolution_bitcast_fusion.2
  263.5 59.5 %reduce-scatter.5.cloned.1.call-done = f32[512,32]{0,1:T(8,128)} async-done(((f32[512,256]{0,1:T(8,128)}), f32[512,32]{0,1:T(8,128)}) %reduce-scatter.5.cloned.1.call-update) | async-done | bytes 65552 | tf_op jit(solution)/shard_map/reduce_scatter | solution.py:70
  323.0 6.0 %all_gather.22 = f32[2048,32]{0,1:T(8,128)S(1)} all-gather(f32[512,32]{0,1:T(8,128)} %reduce-scatter.5.cloned.1.call-done), channel_id=1, replica_groups=mesh['row'=4,'col'=8] {'row'}, dimensions={0}, use_global_device_ids=true | all-gather | bytes 327680 | tf_op jit(solution)/shard_map/all_gather | solution.py:71
  329.6 2.0 fusion.31
  331.6 1.3 collective-permute-start.7
  332.9 7.4 %collective-permute-done.7 = f32[512,32]{0,1:T(8,128)S(1)} collective-permute-done((f32[512,32]{0,1:T(8,128)S(1)}, f32[512,32]{0,1:T(8,128)S(1)}, u32[]{:S(2)}, u32[]{:S(2)}) %collective-permute-start.7) | collective-permute-done | bytes 65568 | tf_op jit(solution)/shard_map/ppermute | solution.py:14
  340.3 7.0 %collective-permute-done.8 = f32[512,32]{0,1:T(8,128)S(1)} collective-permute-done((f32[512,32]{0,1:T(8,128)S(1)}, f32[512,32]{0,1:T(8,128)S(1)}, u32[]{:S(2)}, u32[]{:S(2)}) %collective-permute-start.8) | collective-permute-done | bytes 65568 | tf_op jit(solution)/shard_map/ppermute | solution.py:14
  347.3 7.0 %collective-permute-done.9 = f32[512,32]{0,1:T(8,128)S(1)} collective-permute-done((f32[512,32]{0,1:T(8,128)S(1)}, f32[512,32]{0,1:T(8,128)S(1)}, u32[]{:S(2)}, u32[]{:S(2)}) %collective-permute-start.9) | collective-permute-done | bytes 65568 | tf_op jit(solution)/shard_map/ppermute | solution.py:14
  354.3 8.3 %collective-permute-done.10 = f32[512,32]{0,1:T(8,128)S(1)} collective-permute-done((f32[512,32]{0,1:T(8,128)S(1)}, f32[512,32]{0,1:T(8,128)S(1)}, u32[]{:S(2)}, u32[]{:S(2)}) %collective-permute-start.10) | collective-permute-done | bytes 65568 | tf_op jit(solution)/shard_map/ppermute | solution.py:14
  362.6 8.7 %collective-permute-done.11 = f32[512,32]{0,1:T(8,128)S(1)} collective-permute-done((f32[512,32]{0,1:T(8,128)S(1)}, f32[512,32]{0,1:T(8,128)S(1)}, u32[]{:S(2)}, u32[]{:S(2)}) %collective-permute-start.11) | collective-permute-done | bytes 65568 | tf_op jit(solution)/shard_map/ppermute | solution.py:14
  371.4 8.9 %collective-permute-done.12 = f32[512,32]{0,1:T(8,128)} collective-permute-done((f32[512,32]{0,1:T(8,128)S(1)}, f32[512,32]{0,1:T(8,128)}, u32[]{:S(2)}, u32[]{:S(2)}) %collective-permute-start.12) | collective-permute-done | bytes 65568 | tf_op jit(solution)/shard_map/ppermute | solution.py:14
  380.3 1.3 copy.25
  381.6 2.5 copy.26
  384.1 3.4 collective-permute-done.13
  387.6 1.5 constant_dynamic-update-slice_fusion.15
  389.0 1.5 constant_dynamic-update-slice_fusion.14
  394.3 3.0 copy.28
  397.3 3.2 gather_fusion.2
  400.5 3.4 convolution_bitcast_fusion.4
  403.9 1.7 fusion.27
  405.6 48.4 %all-gather.11.cloned.1.call-done = bf16[8192,256]{0,1:T(8,128)(2,1)} async-done(((bf16[1024,256]{0,1:T(8,128)(2,1)}), bf16[8192,256]{0,1:T(8,128)(2,1)}) %all-gather.11.cloned.1.call-update) | async-done | bytes 4194320 | tf_op jit(solution)/shard_map/all_gather | solution.py:53
  454.0 6.4 %copy.29 = bf16[8192,256]{1,0:T(8,128)(2,1)} copy(bf16[8192,256]{0,1:T(8,128)(2,1)} %all-gather.11.cloned.1.call-done) | data formatting | bytes 8388608 | tf_op jit(solution)/shard_map/while | solution.py:62
  460.5 45.6 %while.21 = (s32[]{:T(128)}, f32[1024,256]{1,0:T(8,128)S(1)}, s32[]{:T(128)}, bf16[8,1024,1024]{2,1,0:T(8,128)(2,1)}, s32[8]{0:T(128)S(1)}, /*index=5*/bf16[8,10...) while((s32[]{:T(128)}, f32[1024,256]{1,0:T(8,128)S(1)}, s32[]{:T(128)}, ...), condition=%wide.region_5.7_spmd, body=%wide.region_4.6_spmd.sunk | while | flops 537133056 | bytes 4718773 | solution.py:62
  463.7 2.4 fusion.76
  469.3 2.4 fusion.76
  475.0 2.4 fusion.76
  480.6 2.4 fusion.76
  486.2 2.4 fusion.76
  491.8 2.4 fusion.76
  497.5 2.4 fusion.76
  503.1 2.4 fusion.76
  506.2 1.3 copy.24
  507.5 2.9 fusion.25
  510.4 1.3 copy.27
  (93 shorter events, 17.0 us)
Async XLA Ops:
  7.2 77.6 %copy-start = (f32[1,2,512,512]{3,2,1,0:T(8,128)S(1)}, f32[1,2,512,512]{3,2,1,0:T(8,128)}, u32[]{:S(2)}) copy-start(f32[1,2,512,512]{3,2,1,0:T(8,128)} %param.27) | copy-start | bytes 6291460
  7.2 71.0 %reduce-scatter.3.cloned.1.call-start = ((), (), s32[]{:S(2)}) async-start(), calls=%async_computation.3 | async-start | bytes 589824 | tf_op jit(solution)/shard_map/reduce_scatter | solution.py:70
  8.0 6.9 %copy-start.2 = (f32[1024,256]{1,0:T(8,128)S(1)}, f32[1024,256]{1,0:T(8,128)}, u32[]{:S(2)}) copy-start(f32[1024,256]{1,0:T(8,128)} %param.17) | copy-start | bytes 3145732
  11.5 2.7 copy-start.8
  11.5 4.3 copy-start.10
  14.1 128.3 %all-gather.5.cloned.1.call-start = ((), (), s32[]{:S(2)}) async-start(), calls=%async_computation.2 | async-start | bytes 2359296 | tf_op jit(solution)/shard_map/all_gather | solution.py:64
  14.9 194.0 %all-gather.7.cloned.1.call-start = ((), (), s32[]{:S(2)}) async-start(), calls=%async_computation.4 | async-start | bytes 4718592 | tf_op jit(solution)/shard_map/all_gather | solution.py:53
  15.8 307.2 %reduce-scatter.5.cloned.1.call-start = ((), (), s32[]{:S(2)}) async-start(), calls=%async_computation.6 | async-start | bytes 589824 | tf_op jit(solution)/shard_map/reduce_scatter | solution.py:70
  15.9 111.2 %copy-start.11 = (s32[1,4]{1,0:T(1,128)S(1)}, s32[1,4]{1,0:T(1,128)}, u32[]{:S(2)}) copy-start(s32[1,4]{1,0:T(1,128)} %param.24) | copy-start | bytes 52
  86.8 8.5 %collective-permute-start = (f32[512,32]{0,1:T(8,128)S(1)}, f32[512,32]{0,1:T(8,128)S(1)}, u32[]{:S(2)}, u32[]{:S(2)}) collective-permute-start(f32[512,32]{0,1:T(8,128)S(1)} %fusion.28), channel_id=1, source_target_pairs={{0,1},{1,2},{2,3},{3,4},{4,5},{5,6},{6,7},{7,0},{8,9},{9,10},{10,1... | collective-permute-start | bytes 196616 | tf_op jit(solution)/shard_map/ppermute | solution.py:14
  95.3 8.1 %collective-permute-start.1 = (f32[512,32]{0,1:T(8,128)S(1)}, f32[512,32]{0,1:T(8,128)S(1)}, u32[]{:S(2)}, u32[]{:S(2)}) collective-permute-start(f32[512,32]{0,1:T(8,128)S(1)} %collective-permute-done), channel_id=1, source_target_pairs={{0,1},{1,2},{2,3},{3,4},{4,5},{5,6},{6,7},{7,0},{8,9},{9,10},{10,1... | collective-permute-start | bytes 196616 | tf_op jit(solution)/shard_map/ppermute | solution.py:14
  103.4 7.0 %collective-permute-start.2 = (f32[512,32]{0,1:T(8,128)S(1)}, f32[512,32]{0,1:T(8,128)S(1)}, u32[]{:S(2)}, u32[]{:S(2)}) collective-permute-start(f32[512,32]{0,1:T(8,128)S(1)} %collective-permute-done.1), channel_id=1, source_target_pairs={{0,1},{1,2},{2,3},{3,4},{4,5},{5,6},{6,7},{7,0},{8,9},{9,10},{10,1... | collective-permute-start | bytes 196616 | tf_op jit(solution)/shard_map/ppermute | solution.py:14
  110.3 8.7 %collective-permute-start.3 = (f32[512,32]{0,1:T(8,128)S(1)}, f32[512,32]{0,1:T(8,128)S(1)}, u32[]{:S(2)}, u32[]{:S(2)}) collective-permute-start(f32[512,32]{0,1:T(8,128)S(1)} %collective-permute-done.2), channel_id=1, source_target_pairs={{0,1},{1,2},{2,3},{3,4},{4,5},{5,6},{6,7},{7,0},{8,9},{9,10},{10,1... | collective-permute-start | bytes 196616 | tf_op jit(solution)/shard_map/ppermute | solution.py:14
  119.0 8.0 %collective-permute-start.4 = (f32[512,32]{0,1:T(8,128)S(1)}, f32[512,32]{0,1:T(8,128)S(1)}, u32[]{:S(2)}, u32[]{:S(2)}) collective-permute-start(f32[512,32]{0,1:T(8,128)S(1)} %collective-permute-done.3), channel_id=1, source_target_pairs={{0,1},{1,2},{2,3},{3,4},{4,5},{5,6},{6,7},{7,0},{8,9},{9,10},{10,1... | collective-permute-start | bytes 196616 | tf_op jit(solution)/shard_map/ppermute | solution.py:14
  127.0 8.2 %collective-permute-start.5 = (f32[512,32]{0,1:T(8,128)S(1)}, f32[512,32]{0,1:T(8,128)S(1)}, u32[]{:S(2)}, u32[]{:S(2)}) collective-permute-start(f32[512,32]{0,1:T(8,128)S(1)} %collective-permute-done.4), channel_id=1, source_target_pairs={{0,1},{1,2},{2,3},{3,4},{4,5},{5,6},{6,7},{7,0},{8,9},{9,10},{10,1... | collective-permute-start | bytes 196616 | tf_op jit(solution)/shard_map/ppermute | solution.py:14
  135.3 7.0 %collective-permute-start.6 = (f32[512,32]{0,1:T(8,128)S(1)}, f32[512,32]{0,1:T(8,128)S(1)}, u32[]{:S(2)}, u32[]{:S(2)}) collective-permute-start(f32[512,32]{0,1:T(8,128)S(1)} %collective-permute-done.5), channel_id=1, source_target_pairs={{0,1},{1,2},{2,3},{3,4},{4,5},{5,6},{6,7},{7,0},{8,9},{9,10},{10,1... | collective-permute-start | bytes 196616 | tf_op jit(solution)/shard_map/ppermute | solution.py:14
  142.4 6.8 %copy-start.5 = (f32[1,256,512]{2,1,0:T(8,128)S(1)}, f32[1,256,512]{2,1,0:T(8,128)}, u32[]{:S(2)}) copy-start(f32[1,256,512]{2,1,0:T(8,128)} %param.23) | copy-start | bytes 1572868
  145.8 63.1 %copy-start.12 = (s32[1,8]{1,0:T(1,128)S(1)}, s32[1,8]{1,0:T(1,128)}, u32[]{:S(2)}) copy-start(s32[1,8]{1,0:T(1,128)} %param.19) | copy-start | bytes 100
  256.0 3.5 copy-start.1
  259.5 1.0 copy-start.4
  259.5 1.4 copy-start.6
  260.9 1.5 copy-start.9
  262.3 132.0 %all-gather.9.cloned.1.call-start = ((), (), s32[]{:S(2)}) async-start(), calls=%async_computation.5 | async-start | bytes 2359296 | tf_op jit(solution)/shard_map/all_gather | solution.py:64
  262.9 191.1 %all-gather.11.cloned.1.call-start = ((), (), s32[]{:S(2)}) async-start(), calls=%async_computation.7 | async-start | bytes 4718592 | tf_op jit(solution)/shard_map/all_gather | solution.py:53
  263.5 116.8 %copy-start.3 = (f32[1024,256]{1,0:T(8,128)S(1)}, f32[1024,256]{1,0:T(8,128)}, u32[]{:S(2)}) copy-start(f32[1024,256]{1,0:T(8,128)} %param.17) | copy-start | bytes 3145732
  331.6 8.7 %collective-permute-start.7 = (f32[512,32]{0,1:T(8,128)S(1)}, f32[512,32]{0,1:T(8,128)S(1)}, u32[]{:S(2)}, u32[]{:S(2)}) collective-permute-start(f32[512,32]{0,1:T(8,128)S(1)} %fusion.31), channel_id=1, source_target_pairs={{0,1},{1,2},{2,3},{3,4},{4,5},{5,6},{6,7},{7,0},{8,9},{9,10},{10,1... | collective-permute-start | bytes 196616 | tf_op jit(solution)/shard_map/ppermute | solution.py:14
  340.3 7.0 %collective-permute-start.8 = (f32[512,32]{0,1:T(8,128)S(1)}, f32[512,32]{0,1:T(8,128)S(1)}, u32[]{:S(2)}, u32[]{:S(2)}) collective-permute-start(f32[512,32]{0,1:T(8,128)S(1)} %collective-permute-done.7), channel_id=1, source_target_pairs={{0,1},{1,2},{2,3},{3,4},{4,5},{5,6},{6,7},{7,0},{8,9},{9,10},{10,1... | collective-permute-start | bytes 196616 | tf_op jit(solution)/shard_map/ppermute | solution.py:14
  347.3 7.0 %collective-permute-start.9 = (f32[512,32]{0,1:T(8,128)S(1)}, f32[512,32]{0,1:T(8,128)S(1)}, u32[]{:S(2)}, u32[]{:S(2)}) collective-permute-start(f32[512,32]{0,1:T(8,128)S(1)} %collective-permute-done.8), channel_id=1, source_target_pairs={{0,1},{1,2},{2,3},{3,4},{4,5},{5,6},{6,7},{7,0},{8,9},{9,10},{10,1... | collective-permute-start | bytes 196616 | tf_op jit(solution)/shard_map/ppermute | solution.py:14
  354.3 8.3 %collective-permute-start.10 = (f32[512,32]{0,1:T(8,128)S(1)}, f32[512,32]{0,1:T(8,128)S(1)}, u32[]{:S(2)}, u32[]{:S(2)}) collective-permute-start(f32[512,32]{0,1:T(8,128)S(1)} %collective-permute-done.9), channel_id=1, source_target_pairs={{0,1},{1,2},{2,3},{3,4},{4,5},{5,6},{6,7},{7,0},{8,9},{9,10},{10,1... | collective-permute-start | bytes 196616 | tf_op jit(solution)/shard_map/ppermute | solution.py:14
  362.6 8.7 %collective-permute-start.11 = (f32[512,32]{0,1:T(8,128)S(1)}, f32[512,32]{0,1:T(8,128)S(1)}, u32[]{:S(2)}, u32[]{:S(2)}) collective-permute-start(f32[512,32]{0,1:T(8,128)S(1)} %collective-permute-done.10), channel_id=1, source_target_pairs={{0,1},{1,2},{2,3},{3,4},{4,5},{5,6},{6,7},{7,0},{8,9},{9,10},{10,1... | collective-permute-start | bytes 196616 | tf_op jit(solution)/shard_map/ppermute | solution.py:14
  371.4 8.9 %collective-permute-start.12 = (f32[512,32]{0,1:T(8,128)S(1)}, f32[512,32]{0,1:T(8,128)}, u32[]{:S(2)}, u32[]{:S(2)}) collective-permute-start(f32[512,32]{0,1:T(8,128)S(1)} %collective-permute-done.11), channel_id=1, source_target_pairs={{0,1},{1,2},{2,3},{3,4},{4,5},{5,6},{6,7},{7,0},{8,9},{9,10},{10,1... | collective-permute-start | bytes 196616 | tf_op jit(solution)/shard_map/ppermute | solution.py:14
  380.3 7.3 %collective-permute-start.13 = (f32[512,32]{0,1:T(8,128)}, f32[512,32]{0,1:T(8,128)}, u32[]{:S(2)}, u32[]{:S(2)}) collective-permute-start(f32[512,32]{0,1:T(8,128)} %collective-permute-done.12), channel_id=1, source_target_pairs={{0,1},{1,2},{2,3},{3,4},{4,5},{5,6},{6,7},{7,0},{8,9},{9,10},{10,1... | collective-permute-start | bytes 196616 | tf_op jit(solution)/shard_map/ppermute | solution.py:14
  397.3 6.6 %copy-start.7 = (f32[1,256,512]{2,1,0:T(8,128)S(1)}, f32[1,256,512]{2,1,0:T(8,128)}, u32[]{:S(2)}) copy-start(f32[1,256,512]{2,1,0:T(8,128)} %param.23) | copy-start | bytes 1572868
Sparse Core Ops, SparseCore 0:
  14.2 63.9 reduce-scatter.2
  80.3 52.4 all-gather.4
  135.6 73.1 all-gather.6
  262.4 60.5 reduce-scatter.4
  324.9 54.2 all-gather.8
  381.3 72.7 all-gather.10
